TPU v7x, 32 devices: a whole 2x2x4 slice. The times are simulated.
32 devices in a mesh: paths: 4 (over y, core), factors: 8 (over z, x).
Axes of the slice: x: 2, y: 2, z: 4, core: 2. Of those that a mesh axis runs over, the one named last changes fastest.
Arguments:
- x_start: float32 [512, 2048], P('factors', 'paths'), may hold values from -3 to 3
- shocks: float32 [4, 512, 2048], P(None, 'factors', 'paths'), may hold values from -6 to 6
- cholesky: float32 [512, 512], P(None, 'factors'), as said below
- reversion: float32 [512], P('factors'), may hold values from 0.05 to 2
- sabr_alpha: float32 [64], replicated, may hold values from 0.2 to 0.6
- sabr_rho: float32 [64], replicated, may hold values from -0.7 to 0.7
- sabr_nu: float32 [64], replicated, may hold values from 0.3 to 1.5
- factor_slice: int32 [512], P('factors'), may hold values from 0 to 63
- notional: float32 [32768], P('factors'), may hold values from -1 to 1
- strike: float32 [32768], P('factors'), may hold values from -3 to 3
- trade_set: int32 [32768], P('factors'), may hold values from 0 to 255
- trade_factor: int32 [32768], P('factors'), may hold values from 0 to 511, as said below
- loss_given: float32 [256], replicated, may hold values from 0.2 to 0.8
Outputs:
- path_adjoint: float32 [512, 2048], P('factors', 'paths')
- sabr_grad: float32 [3, 64], replicated
Inputs may be any that keep to these rules, and one draw needn't show every extreme that they name: `cholesky`: lower triangular with a positive diagonal and rows of unit length. `trade_factor`: trade t's factor lies in [(t // 4096) * 64, (t // 4096 + 1) * 64).
All inputs are finite; a program needn't handle non-finite values.
Results may differ from a plain program's by a relative error of at most 0.004.
Values may be sent and summed in bfloat16 or wider, within the bound.
A program may use at most 192 MiB of HBM per device.

v0:
```python
import math
import jax
import jax.numpy as jnp
from jax import lax
from jax.sharding import PartitionSpec as P

TIME_STEP = 0.25
ROOT_STEP = 0.5
DISCOUNT_RATE = 0.03
PRECISE = lax.Precision.HIGHEST
CONTRACT_FIRST = (((0,), (0,)), ((), ()))


def shortened(value):
    return jax.tree.map(lambda a: a.astype(jnp.bfloat16) if a.dtype == jnp.float32 else a, value)


def smile_terms(squashed, alpha_rows, rho_rows, nu_rows):
    curve = (2.0 - 3.0 * rho_rows * rho_rows) * nu_rows * nu_rows / 24.0
    base = 1.0 + 0.5 * rho_rows * nu_rows * squashed + curve * squashed * squashed
    rho_slope = alpha_rows * (
        0.5 * nu_rows * squashed - 0.25 * rho_rows * nu_rows * nu_rows * squashed * squashed
    )
    nu_slope = alpha_rows * (
        0.5 * rho_rows * squashed
        + (2.0 - 3.0 * rho_rows * rho_rows) * nu_rows * squashed * squashed / 12.0
    )
    level_slope = alpha_rows * (0.5 * rho_rows * nu_rows + 2.0 * curve * squashed)
    return (alpha_rows * base, base, rho_slope, nu_slope, level_slope)


def split_factors(
    x_start,
    shocks,
    cholesky,
    reversion,
    sabr_alpha,
    sabr_rho,
    sabr_nu,
    factor_slice,
    notional,
    strike,
    trade_set,
    trade_factor,
    loss_given,
):
    factor_rows, path_cols = x_start.shape
    step_count = shocks.shape[0]
    total_sets = loss_given.shape[0]
    factor_place = lax.axis_index("factors")
    slice_count = sabr_alpha.shape[0]
    slice_table = (
        factor_slice[:, None] == jnp.arange(slice_count, dtype=jnp.int32)[None, :]
    ).astype(jnp.float32)
    alpha_rows = jnp.dot(slice_table, sabr_alpha, precision=PRECISE)[:, None]
    rho_rows = jnp.dot(slice_table, sabr_rho, precision=PRECISE)[:, None]
    nu_rows = jnp.dot(slice_table, sabr_nu, precision=PRECISE)[:, None]
    local_factor = trade_factor - factor_place * factor_rows
    factor_table = (
        jnp.arange(factor_rows, dtype=jnp.int32)[:, None] == local_factor[None, :]
    ).astype(jnp.float32)
    set_table = (jnp.arange(total_sets, dtype=jnp.int32)[:, None] == trade_set[None, :]).astype(
        jnp.bfloat16
    )
    damping = (1.0 - reversion * TIME_STEP)[:, None]
    state = x_start
    states = [state]
    weights = []
    for step_index in range(step_count):
        squashed = jnp.tanh(state)
        local_vol = smile_terms(squashed, alpha_rows, rho_rows, nu_rows)[0]
        correlate_source = local_vol * shocks[step_index]
        mixed = lax.psum_scatter(
            jnp.dot(cholesky, correlate_source, precision=PRECISE),
            "factors",
            scatter_dimension=0,
            tiled=True,
        )
        state = damping * state + ROOT_STEP * mixed
        states.append(state)
        moneyness = jnp.take(state, local_factor, axis=0) - strike[:, None]
        values = (notional[:, None] * jnp.tanh(moneyness)).astype(jnp.bfloat16)
        discount = math.exp(-DISCOUNT_RATE * TIME_STEP * (step_index + 1))
        partial_sum = jnp.dot(set_table, values, preferred_element_type=jnp.float32)
        exposure = lax.psum(partial_sum.astype(jnp.bfloat16), "factors").astype(jnp.float32)
        weights.append(
            (discount * loss_given[:, None] * jax.nn.sigmoid(exposure)).astype(jnp.bfloat16)
        )
    adjoint = jnp.zeros_like(x_start)
    factor_sums = jnp.zeros((3, factor_rows), jnp.float32)
    for step_index in reversed(range(step_count)):
        moneyness = jnp.take(states[step_index + 1], local_factor, axis=0) - strike[:, None]
        squash_trade = jnp.tanh(moneyness)
        trade_term = (
            notional[:, None]
            * (1.0 - squash_trade * squash_trade)
            * lax.dot_general(
                set_table, weights[step_index], CONTRACT_FIRST, preferred_element_type=jnp.float32
            )
        )
        adjoint = adjoint + jnp.dot(factor_table, trade_term, precision=PRECISE)
        shock_adjoint = jnp.zeros((factor_rows, path_cols), jnp.float32) + lax.dot_general(
            cholesky,
            lax.all_gather(shortened(ROOT_STEP * adjoint), "factors", axis=0, tiled=True),
            CONTRACT_FIRST,
            precision=PRECISE,
        )
        squashed = jnp.tanh(states[step_index])
        local_vol, base, rho_slope, nu_slope, level_slope = smile_terms(
            squashed, alpha_rows, rho_rows, nu_rows
        )
        vol_adjoint = shock_adjoint * shocks[step_index]
        factor_sums = factor_sums + jnp.stack(
            [
                jnp.sum(vol_adjoint * base, axis=1),
                jnp.sum(vol_adjoint * rho_slope, axis=1),
                jnp.sum(vol_adjoint * nu_slope, axis=1),
            ]
        )
        adjoint = damping * adjoint + vol_adjoint * level_slope * (1.0 - squashed * squashed)
    slice_sums = jnp.dot(factor_sums, slice_table, precision=PRECISE)
    return (adjoint, slice_sums)


def per_device(
    x_start,
    shocks,
    cholesky,
    reversion,
    sabr_alpha,
    sabr_rho,
    sabr_nu,
    factor_slice,
    notional,
    strike,
    trade_set,
    trade_factor,
    loss_given,
):
    adjoint, slice_sums = split_factors(
        x_start,
        shocks,
        cholesky,
        reversion,
        sabr_alpha,
        sabr_rho,
        sabr_nu,
        factor_slice,
        notional,
        strike,
        trade_set,
        trade_factor,
        loss_given,
    )
    total_grad = lax.psum(slice_sums, ("paths", "factors"))
    sabr_grad = total_grad / (x_start.shape[1] * lax.axis_size("paths"))
    return (adjoint, sabr_grad)


def solution(mesh):
    return jax.shard_map(
        per_device,
        mesh=mesh,
        in_specs=(
            P("factors", "paths"),
            P(None, "factors", "paths"),
            P(None, "factors"),
            P("factors"),
            P(),
            P(),
            P(),
            P("factors"),
            P("factors"),
            P("factors"),
            P("factors"),
            P("factors"),
            P(),
        ),
        out_specs=(P("factors", "paths"), P()),
        check_vma=False,
    )
```

profile of v0, /device:TPU:0, one launch (start us, length us, event | category | flops | bytes accessed | tf_op | source)
XLA Modules:
  0.0 588.1 jit_solution(14679514657513539477)
XLA Ops:
  10.0 2.1 convolution_bitcast_fusion.3
  12.1 1.3 copy.39
  14.2 66.8 %reduce-scatter.13.cloned.1.call-done = f32[64,512]{1,0:T(8,128)} async-done(((f32[512,512]{1,0:T(8,128)}), f32[64,512]{1,0:T(8,128)}) %reduce-scatter.13.cloned.1.call-update) | async-done | bytes 131088 | tf_op jit(solution)/shard_map/reduce_scatter | solution.py:73
  82.0 2.0 convolution_bitcast_fusion.2
  85.4 63.6 %reduce-scatter.15.cloned.1.call-done = f32[64,512]{1,0:T(8,128)} async-done(((f32[512,512]{1,0:T(8,128)}), f32[64,512]{1,0:T(8,128)}) %reduce-scatter.15.cloned.1.call-update) | async-done | bytes 131088 | tf_op jit(solution)/shard_map/reduce_scatter | solution.py:73
  151.1 1.4 copy.43
  152.7 16.8 %gather_fusion.3 = f32[4096,512]{1,0:T(8,128)} fusion(f32[64,512]{1,0:T(8,128)S(1)} %multiply_add_fusion.4, s32[4096]{0:T(1024)S(1)} %fusion.166), kind=kCustom, calls=%fused_computation.3.clone | custom fusion | bytes 16793600 | tf_op jit(solution)/shard_map/jit(_take)/gather | solution.py:92
  169.5 46.4 %reduce-scatter.17.cloned.1.call-done = f32[64,512]{1,0:T(8,128)} async-done(((f32[512,512]{1,0:T(8,128)}), f32[64,512]{1,0:T(8,128)}) %reduce-scatter.17.cloned.1.call-update) | async-done | bytes 131088 | tf_op jit(solution)/shard_map/reduce_scatter | solution.py:73
  218.0 1.4 copy.45
  219.8 6.3 %fusion.67 = bf16[256,512]{1,0:T(8,128)(2,1)} fusion(f32[4096,512]{1,0:T(8,128)} %gather_fusion.3, f32[4096]{0:T(1024)S(1)} %copy-done.10, f32[4096]{0:T(1024)S(1)} %copy-done.11, pred[4096]{0:T(1024)(128)(4,1)S(1)} %get-tuple-element.32, s32[4096]{0:T(1024)S(1)} %copy-done.3), kind=kOutput, calls=%fused_computation.80 | convolution fusion | flops 1083310080 | bytes 8704000 | tf_op jit(solution)/shard_map/dot_general | solution.py:84
  226.1 16.8 %gather_fusion.2 = f32[4096,512]{1,0:T(8,128)} fusion(f32[64,512]{1,0:T(8,128)S(1)} %multiply_add_fusion.3, s32[4096]{0:T(1024)S(1)} %fusion.166), kind=kCustom, calls=%fused_computation.2.clone | custom fusion | bytes 16793600 | tf_op jit(solution)/shard_map/jit(_take)/gather | solution.py:92
  242.9 6.3 %fusion.66 = bf16[256,512]{1,0:T(8,128)(2,1)} fusion(f32[4096,512]{1,0:T(8,128)} %gather_fusion.2, f32[4096]{0:T(1024)S(1)} %copy-done.10, f32[4096]{0:T(1024)S(1)} %copy-done.11, pred[4096]{0:T(1024)(128)(4,1)S(1)} %get-tuple-element.32, s32[4096]{0:T(1024)S(1)} %copy-done.3), kind=kOutput, calls=%fused_computation.79 | convolution fusion | flops 1083310080 | bytes 8704000 | tf_op jit(solution)/shard_map/dot_general | solution.py:84
  249.2 16.8 %gather_fusion.1 = f32[4096,512]{1,0:T(8,128)} fusion(f32[64,512]{1,0:T(8,128)S(1)} %multiply_add_fusion.2, s32[4096]{0:T(1024)S(1)} %fusion.166), kind=kCustom, calls=%fused_computation.1.clone | custom fusion | bytes 16793600 | tf_op jit(solution)/shard_map/jit(_take)/gather | solution.py:92
  266.0 6.4 %fusion.65 = bf16[256,512]{1,0:T(8,128)(2,1)} fusion(f32[4096,512]{1,0:T(8,128)} %gather_fusion.1, f32[4096]{0:T(1024)S(1)} %copy-done.10, f32[4096]{0:T(1024)S(1)} %copy-done.11, pred[4096]{0:T(1024)(128)(4,1)S(1)} %get-tuple-element.32, s32[4096]{0:T(1024)S(1)} %copy-done.3), kind=kOutput, calls=%fused_computation.78 | convolution fusion | flops 1083310080 | bytes 8704000 | tf_op jit(solution)/shard_map/dot_general | solution.py:84
  272.3 10.4 %reduce-scatter.19.cloned.1.call-done = f32[64,512]{1,0:T(8,128)} async-done(((f32[512,512]{1,0:T(8,128)}), f32[64,512]{1,0:T(8,128)}) %reduce-scatter.19.cloned.1.call-update) | async-done | bytes 131088 | tf_op jit(solution)/shard_map/reduce_scatter | solution.py:73
  283.7 16.8 %gather_fusion = f32[4096,512]{1,0:T(8,128)} fusion(f32[64,512]{1,0:T(8,128)S(1)} %multiply_add_fusion.1, s32[4096]{0:T(1024)S(1)} %fusion.166), kind=kCustom, calls=%fused_computation.clone | custom fusion | bytes 16793600 | tf_op jit(solution)/shard_map/jit(_take)/gather | solution.py:92
  300.5 6.3 %fusion.64 = bf16[256,512]{1,0:T(8,128)(2,1)} fusion(f32[4096,512]{1,0:T(8,128)} %gather_fusion, f32[4096]{0:T(1024)S(1)} %copy-done.10, f32[4096]{0:T(1024)S(1)} %copy-done.11, pred[4096]{0:T(1024)(128)(4,1)S(1)} %get-tuple-element.32, s32[4096]{0:T(1024)S(1)} %copy-done.3), kind=kOutput, calls=%fused_computation.77 | convolution fusion | flops 1083310080 | bytes 8704000 | tf_op jit(solution)/shard_map/dot_general | solution.py:84
  306.9 77.6 %all-reduce.3.cloned.1.call-done = (bf16[256,512]{1,0:T(8,128)(2,1)}, bf16[256,512]{1,0:T(8,128)(2,1)}, bf16[256,512]{1,0:T(8,128)(2,1)}, bf16[256,512]{1,0:T(8,128)(2,1)}) async-done(((bf16[256,512]{1,0:T(8,128)(2,1)}, bf16[256,512]{1,0:T(8,128)(2,1)}, bf16[256,512]{1,0:T(8,128)(2,1)}, bf16[256,512]{1,0:T(8,128)(2,1)}), (bf16[256,512]{1,0:T(8,128)(2,1)}, bf16[256,512]{1,0:T(8,128)(2,1)}, ...) | async-done | bytes 1048592 | tf_op jit(solution)/shard_map/psum | solution.py:85
  384.5 2.5 fusion.38
  387.9 5.4 multiply_convert_fusion.27
  393.3 31.8 %all_gather.12 = bf16[512,512]{1,0:T(8,128)(2,1)S(1)} all-gather(bf16[64,512]{1,0:T(8,128)(2,1)S(1)} %get-tuple-element.45), channel_id=1, replica_groups=mesh['paths'=4,'factors'=8] {'factors'}, dimensions={0}, use_global_device_ids=true | all-gather | bytes 589824 | tf_op jit(solution)/shard_map/all_gather | solution.py:104
  425.5 1.4 fusion.36
  427.0 5.4 multiply_convert_fusion.26
  432.3 31.6 %all_gather.13 = bf16[512,512]{1,0:T(8,128)(2,1)S(1)} all-gather(bf16[64,512]{1,0:T(8,128)(2,1)S(1)} %get-tuple-element.47), channel_id=1, replica_groups=mesh['paths'=4,'factors'=8] {'factors'}, dimensions={0}, use_global_device_ids=true | all-gather | bytes 589824 | tf_op jit(solution)/shard_map/all_gather | solution.py:104
  464.3 1.4 fusion.34
  465.8 5.4 multiply_convert_fusion.25
  471.2 31.5 %all_gather.14 = bf16[512,512]{1,0:T(8,128)(2,1)S(1)} all-gather(bf16[64,512]{1,0:T(8,128)(2,1)S(1)} %get-tuple-element.49), channel_id=1, replica_groups=mesh['paths'=4,'factors'=8] {'factors'}, dimensions={0}, use_global_device_ids=true | all-gather | bytes 589824 | tf_op jit(solution)/shard_map/all_gather | solution.py:104
  503.1 1.4 fusion.32
  504.5 5.4 multiply_convert_fusion.24
  509.9 31.2 %all_gather.15 = bf16[512,512]{1,0:T(8,128)(2,1)S(1)} all-gather(bf16[64,512]{1,0:T(8,128)(2,1)S(1)} %get-tuple-element.51), channel_id=1, replica_groups=mesh['paths'=4,'factors'=8] {'factors'}, dimensions={0}, use_global_device_ids=true | all-gather | bytes 589824 | tf_op jit(solution)/shard_map/all_gather | solution.py:104
  541.1 1.6 fusion.100
  542.9 37.8 %psum.39 = f32[3,64]{1,0:T(4,128)S(1)} all-reduce(f32[3,64]{1,0:T(4,128)S(1)} %fusion.161), channel_id=1, replica_groups=mesh['paths'=4,'factors'=8] {'paths','factors'}, use_global_device_ids=true, to_apply=%region_20.22 | all-reduce | flops 192 | bytes 1536 | tf_op jit(solution)/shard_map/psum | solution.py:155
  (71 shorter events, 14.6 us)
Async XLA Ops:
  7.2 2.8 copy-start
  7.2 142.8 %copy-start.2 = (f32[4,64,512]{2,1,0:T(8,128)S(1)}, f32[4,64,512]{2,1,0:T(8,128)}, u32[]{:S(2)}) copy-start(f32[4,64,512]{2,1,0:T(8,128)} %param.16) | copy-start | bytes 1572868
  7.2 145.4 %copy-start.8 = (s32[4096]{0:T(1024)S(1)}, s32[4096]{0:T(1024)}, u32[]{:S(2)}) copy-start(s32[4096]{0:T(1024)} %param.26) | copy-start | bytes 49156
  7.2 73.7 %reduce-scatter.13.cloned.1.call-start = ((), (), s32[]{:S(2)}) async-start(), calls=%async_computation.4 | async-start | bytes 1179648 | tf_op jit(solution)/shard_map/reduce_scatter | solution.py:73
  13.5 135.6 %reduce-scatter.15.cloned.1.call-start = ((), (), s32[]{:S(2)}) async-start(), calls=%async_computation.5 | async-start | bytes 1179648 | tf_op jit(solution)/shard_map/reduce_scatter | solution.py:73
  85.4 130.5 %reduce-scatter.17.cloned.1.call-start = ((), (), s32[]{:S(2)}) async-start(), calls=%async_computation.6 | async-start | bytes 1179648 | tf_op jit(solution)/shard_map/reduce_scatter | solution.py:73
  152.6 130.2 %reduce-scatter.19.cloned.1.call-start = ((), (), s32[]{:S(2)}) async-start(), calls=%async_computation.7 | async-start | bytes 1179648 | tf_op jit(solution)/shard_map/reduce_scatter | solution.py:73
  152.7 67.1 %copy-start.3 = (s32[4096]{0:T(1024)S(1)}, s32[4096]{0:T(1024)}, u32[]{:S(2)}) copy-start(s32[4096]{0:T(1024)} %param.25) | copy-start | bytes 49156
  152.7 67.1 %copy-start.10 = (f32[4096]{0:T(1024)S(1)}, f32[4096]{0:T(1024)}, u32[]{:S(2)}) copy-start(f32[4096]{0:T(1024)} %param.24) | copy-start | bytes 49156
  152.7 67.1 %copy-start.11 = (f32[4096]{0:T(1024)S(1)}, f32[4096]{0:T(1024)}, u32[]{:S(2)}) copy-start(f32[4096]{0:T(1024)} %param.23) | copy-start | bytes 49156
  219.4 165.1 %all-reduce.3.cloned.1.call-start = ((), (), s32[]{:S(2)}) async-start(), calls=%async_computation.8 | async-start | bytes 2097152 | tf_op jit(solution)/shard_map/psum | solution.py:85
  300.5 6.4 %copy-start.9 = (f32[256]{0:T(256)S(1)}, f32[256]{0:T(256)}, u32[]{:S(2)}) copy-start(f32[256]{0:T(256)} %param.27) | copy-start | bytes 3076
  384.5 3.5 copy-start.1
  384.5 42.4 %slice-start.4 = ((s8[8388608]{0:T(1024)(128)(4,1)}), s8[4194304]{0:T(1024)(128)(4,1)S(1)}, s32[]{:S(2)}) async-start(s8[8388608]{0:T(1024)(128)(4,1)} %bitcast.89), calls=%async_computation.13 | async-start | bytes 8388608
  387.9 37.6 %copy-start.7 = (bf16[256,512]{1,0:T(8,128)(2,1)S(1)}, bf16[256,512]{1,0:T(8,128)(2,1)}, u32[]{:S(2)}) copy-start(bf16[256,512]{1,0:T(8,128)(2,1)} %get-tuple-element.28) | copy-start | bytes 786436
  387.9 39.0 %slice-start.5 = ((s8[8388608]{0:T(1024)(128)(4,1)}), s8[4194304]{0:T(1024)(128)(4,1)S(1)}, s32[]{:S(2)}) async-start(s8[8388608]{0:T(1024)(128)(4,1)} %bitcast.89), calls=%async_computation.14 | async-start | bytes 8388608
  426.9 38.8 %slice-start.2 = ((s8[8388608]{0:T(1024)(128)(4,1)}), s8[4194304]{0:T(1024)(128)(4,1)S(1)}, s32[]{:S(2)}) async-start(s8[8388608]{0:T(1024)(128)(4,1)} %bitcast.87), calls=%async_computation.11 | async-start | bytes 8388608
  427.0 37.4 %copy-start.6 = (bf16[256,512]{1,0:T(8,128)(2,1)S(1)}, bf16[256,512]{1,0:T(8,128)(2,1)}, u32[]{:S(2)}) copy-start(bf16[256,512]{1,0:T(8,128)(2,1)} %get-tuple-element.27) | copy-start | bytes 786436
  427.0 38.8 %slice-start.3 = ((s8[8388608]{0:T(1024)(128)(4,1)}), s8[4194304]{0:T(1024)(128)(4,1)S(1)}, s32[]{:S(2)}) async-start(s8[8388608]{0:T(1024)(128)(4,1)} %bitcast.87), calls=%async_computation.12 | async-start | bytes 8388608
  465.7 38.7 %slice-start = ((s8[8388608]{0:T(1024)(128)(4,1)}), s8[4194304]{0:T(1024)(128)(4,1)S(1)}, s32[]{:S(2)}) async-start(s8[8388608]{0:T(1024)(128)(4,1)} %bitcast.85), calls=%async_computation.9 | async-start | bytes 8388608
  465.8 37.3 %copy-start.5 = (bf16[256,512]{1,0:T(8,128)(2,1)S(1)}, bf16[256,512]{1,0:T(8,128)(2,1)}, u32[]{:S(2)}) copy-start(bf16[256,512]{1,0:T(8,128)(2,1)} %get-tuple-element.26) | copy-start | bytes 786436
  465.8 38.7 %slice-start.1 = ((s8[8388608]{0:T(1024)(128)(4,1)}), s8[4194304]{0:T(1024)(128)(4,1)S(1)}, s32[]{:S(2)}) async-start(s8[8388608]{0:T(1024)(128)(4,1)} %bitcast.85), calls=%async_computation.10 | async-start | bytes 8388608
  504.5 36.6 %copy-start.4 = (f32[64,512]{1,0:T(8,128)S(1)}, f32[64,512]{1,0:T(8,128)}, u32[]{:S(2)}) copy-start(f32[64,512]{1,0:T(8,128)} %param.15) | copy-start | bytes 393220
  504.5 38.2 %copy-start.12 = (s32[64]{0:T(128)S(1)}, s32[64]{0:T(128)}, u32[]{:S(2)}) copy-start(s32[64]{0:T(128)} %param.22) | copy-start | bytes 772
Sparse Core Ops, SparseCore 0:
  13.6 67.3 reduce-scatter.12
  85.5 63.4 reduce-scatter.14
  152.7 63.1 reduce-scatter.16
  219.5 63.1 reduce-scatter.18
  307.0 77.4 all-reduce.2
where the time goes:
time: 593 us; the launch traced here: 588 us
  waiting for transfers between devices  265 us (45%)
  blocking collectives  164 us (28%)
  local copies, waits for them, and re-layouts  73.7 us (12%)
  matrix products  65.5 us (11%)
  between operations  14.4 us (2%)
    reduce_scatter x4, waiting for transfers between devices, split_factors(): lax.psum_scatter(jnp.dot(cholesky, correlate_source, precision=PRECISE),...  187 us
    all_gather x4, blocking collectives, split_factors(): lax.all_gather(shortened(ROOT_STEP * adjoint), 'factors', axis=0, tiled=T...  126 us
    psum x1, waiting for transfers between devices, split_factors(): lax.psum(partial_sum.astype(jnp.bfloat16), 'factors').astype(jnp.float32)  77.6 us
    gather x4, local copies, waits for them, and re-layouts, split_factors(): jnp.take(states[step_index + 1], local_factor, axis=0) - strike[:, None]  67.2 us
    psum x1, blocking collectives, per_device(): total_grad = lax.psum(slice_sums, ('paths', 'factors'))  37.8 us
    dot_general x4, matrix products, split_factors(): partial_sum = jnp.dot(set_table, values, preferred_element_type=jnp.float32)  25.3 us
    dot_general x4, matrix products, split_factors(): adjoint = adjoint + jnp.dot(factor_table, trade_term, precision=PRECISE)  21.5 us
  transfers between devices with their start and end apart: 5, of which 5 were waited for; matrix products, arithmetic and copies ran while one was open for 12% of the time, Pallas kernels for 0%

commit v1 on v0

--- a/solution.py
+++ b/solution.py
@@ -9,6 +9,11 @@
 DISCOUNT_RATE = 0.03
 PRECISE = lax.Precision.HIGHEST
 CONTRACT_FIRST = (((0,), (0,)), ((), ()))
+
+
+def gather_by_exchange(array, axis, dim):
+    copies = jnp.concatenate([array] * lax.axis_size(axis), axis=dim)
+    return lax.all_to_all(copies, axis, dim, dim, tiled=True)
 
 
 def shortened(value):
@@ -101,7 +106,7 @@
         adjoint = adjoint + jnp.dot(factor_table, trade_term, precision=PRECISE)
         shock_adjoint = jnp.zeros((factor_rows, path_cols), jnp.float32) + lax.dot_general(
             cholesky,
-            lax.all_gather(shortened(ROOT_STEP * adjoint), "factors", axis=0, tiled=True),
+            gather_by_exchange(shortened(ROOT_STEP * adjoint), "factors", 0),
             CONTRACT_FIRST,
             precision=PRECISE,
         )

time: 593 us -> 558 us (0.941)
  blocking collectives: 164 us -> 56.9 us
  waiting for transfers between devices: 265 us -> 294 us
  matrix products: 65.5 us -> 88.5 us
  local copies, waits for them, and re-layouts: 73.7 us -> 86.8 us
  starting transfers between devices: 0.5 us -> 11.7 us
    all_gather x4 -> x0, blocking collectives: 126 us -> none  [split_factors(): lax.all_gather(shortened(ROOT_STEP * adjoint), 'factors', axis=0, tiled=T...]
    all_to_all x0 -> x3, waiting for transfers between devices: none -> 29.2 us  [gather_by_exchange(): return lax.all_to_all(copies, axis, dim, dim, tiled=True)]
    all_to_all x0 -> x1, blocking collectives: none -> 18.1 us  [gather_by_exchange(): return lax.all_to_all(copies, axis, dim, dim, tiled=True)]
    dot_general x4, matrix products: 21.5 us -> 34.9 us  [split_factors(): adjoint = adjoint + jnp.dot(factor_table, trade_term, precision=PRECISE)]
    all_to_all x0 -> x3, starting transfers between devices: none -> 11.3 us  [gather_by_exchange(): return lax.all_to_all(copies, axis, dim, dim, tiled=True)]
    unnamed x42 -> x54, local copies, waits for them, and re-layouts: 6.53 us -> 17.7 us
    dot_general x4, matrix products: 6.62 us -> 16.3 us  [split_factors(): lax.dot_general(set_table, weights[step_index], CONTRACT_FIRST, preferred...]
  transfers between devices with their start and end apart: 5 -> 8, of which waited for: 5 -> 8; matrix products, arithmetic and copies ran while one was open for 12% -> 15% of each run, Pallas kernels for 0% -> 0%
where the time goes in v1:
time: 558 us; the launch traced here: 557 us
  waiting for transfers between devices  294 us (53%)
  matrix products  88.5 us (16%)
  local copies, waits for them, and re-layouts  86.8 us (16%)
  blocking collectives  56.9 us (10%)
  between operations  14.1 us (3%)
  starting transfers between devices  11.7 us (2%)
    reduce_scatter x4, waiting for transfers between devices, split_factors(): lax.psum_scatter(jnp.dot(cholesky, correlate_source, precision=PRECISE),...  187 us
    psum x1, waiting for transfers between devices, split_factors(): lax.psum(partial_sum.astype(jnp.bfloat16), 'factors').astype(jnp.float32)  77.5 us
    gather x4, local copies, waits for them, and re-layouts, split_factors(): jnp.take(states[step_index + 1], local_factor, axis=0) - strike[:, None]  67.2 us
    psum x1, blocking collectives, per_device(): total_grad = lax.psum(slice_sums, ('paths', 'factors'))  38.7 us
    dot_general x4, matrix products, split_factors(): adjoint = adjoint + jnp.dot(factor_table, trade_term, precision=PRECISE)  34.9 us
    all_to_all x3, waiting for transfers between devices, gather_by_exchange(): return lax.all_to_all(copies, axis, dim, dim, tiled=True)  29.2 us
    dot_general x4, matrix products, split_factors(): partial_sum = jnp.dot(set_table, values, preferred_element_type=jnp.float32)  25.3 us
    all_to_all x1, blocking collectives, gather_by_exchange(): return lax.all_to_all(copies, axis, dim, dim, tiled=True)  18.1 us
  transfers between devices with their start and end apart: 8, of which 8 were waited for; matrix products, arithmetic and copies ran while one was open for 15% of the time, Pallas kernels for 0%

profile of v1, /device:TPU:0, one launch (start us, length us, event | category | flops | bytes accessed | tf_op | source)
XLA Modules:
  0.0 557.0 jit_solution(15462284969064848836)
XLA Ops:
  10.0 2.1 convolution_bitcast_fusion.3
  14.2 66.6 %reduce-scatter.13.cloned.1.call-done = f32[64,512]{1,0:T(8,128)} async-done(((f32[512,512]{1,0:T(8,128)}), f32[64,512]{1,0:T(8,128)}) %reduce-scatter.13.cloned.1.call-update) | async-done | bytes 131088 | tf_op jit(solution)/shard_map/reduce_scatter | solution.py:78
  81.8 2.0 convolution_bitcast_fusion.2
  85.3 63.5 %reduce-scatter.15.cloned.1.call-done = f32[64,512]{1,0:T(8,128)} async-done(((f32[512,512]{1,0:T(8,128)}), f32[64,512]{1,0:T(8,128)}) %reduce-scatter.15.cloned.1.call-update) | async-done | bytes 131088 | tf_op jit(solution)/shard_map/reduce_scatter | solution.py:78
  152.5 16.8 %gather_fusion.3 = f32[4096,512]{1,0:T(8,128)} fusion(f32[64,512]{1,0:T(8,128)S(1)} %multiply_add_fusion.4, s32[4096]{0:T(1024)S(1)} %fusion.166), kind=kCustom, calls=%fused_computation.3.clone | custom fusion | bytes 16793600 | tf_op jit(solution)/shard_map/jit(_take)/gather | solution.py:97
  169.3 46.4 %reduce-scatter.17.cloned.1.call-done = f32[64,512]{1,0:T(8,128)} async-done(((f32[512,512]{1,0:T(8,128)}), f32[64,512]{1,0:T(8,128)}) %reduce-scatter.17.cloned.1.call-update) | async-done | bytes 131088 | tf_op jit(solution)/shard_map/reduce_scatter | solution.py:78
  219.5 6.3 %fusion.67 = bf16[256,512]{1,0:T(8,128)(2,1)} fusion(f32[4096,512]{1,0:T(8,128)} %gather_fusion.3, f32[4096]{0:T(1024)S(1)} %copy-done.10, f32[4096]{0:T(1024)S(1)} %copy-done.11, pred[4096]{0:T(1024)(128)(4,1)S(1)} %get-tuple-element.42, s32[4096]{0:T(1024)S(1)} %copy-done.3), kind=kOutput, calls=%fused_computation.80 | convolution fusion | flops 1083310080 | bytes 8704000 | tf_op jit(solution)/shard_map/dot_general | solution.py:89
  225.8 16.8 %gather_fusion.2 = f32[4096,512]{1,0:T(8,128)} fusion(f32[64,512]{1,0:T(8,128)S(1)} %multiply_add_fusion.3, s32[4096]{0:T(1024)S(1)} %fusion.166), kind=kCustom, calls=%fused_computation.2.clone | custom fusion | bytes 16793600 | tf_op jit(solution)/shard_map/jit(_take)/gather | solution.py:97
  242.6 6.3 %fusion.66 = bf16[256,512]{1,0:T(8,128)(2,1)} fusion(f32[4096,512]{1,0:T(8,128)} %gather_fusion.2, f32[4096]{0:T(1024)S(1)} %copy-done.10, f32[4096]{0:T(1024)S(1)} %copy-done.11, pred[4096]{0:T(1024)(128)(4,1)S(1)} %get-tuple-element.42, s32[4096]{0:T(1024)S(1)} %copy-done.3), kind=kOutput, calls=%fused_computation.79 | convolution fusion | flops 1083310080 | bytes 8704000 | tf_op jit(solution)/shard_map/dot_general | solution.py:89
  248.9 16.8 %gather_fusion.1 = f32[4096,512]{1,0:T(8,128)} fusion(f32[64,512]{1,0:T(8,128)S(1)} %multiply_add_fusion.2, s32[4096]{0:T(1024)S(1)} %fusion.166), kind=kCustom, calls=%fused_computation.1.clone | custom fusion | bytes 16793600 | tf_op jit(solution)/shard_map/jit(_take)/gather | solution.py:97
  265.7 6.4 %fusion.65 = bf16[256,512]{1,0:T(8,128)(2,1)} fusion(f32[4096,512]{1,0:T(8,128)} %gather_fusion.1, f32[4096]{0:T(1024)S(1)} %copy-done.10, f32[4096]{0:T(1024)S(1)} %copy-done.11, pred[4096]{0:T(1024)(128)(4,1)S(1)} %get-tuple-element.42, s32[4096]{0:T(1024)S(1)} %copy-done.3), kind=kOutput, calls=%fused_computation.78 | convolution fusion | flops 1083310080 | bytes 8704000 | tf_op jit(solution)/shard_map/dot_general | solution.py:89
  272.0 10.4 %reduce-scatter.19.cloned.1.call-done = f32[64,512]{1,0:T(8,128)} async-done(((f32[512,512]{1,0:T(8,128)}), f32[64,512]{1,0:T(8,128)}) %reduce-scatter.19.cloned.1.call-update) | async-done | bytes 131088 | tf_op jit(solution)/shard_map/reduce_scatter | solution.py:78
  283.4 16.8 %gather_fusion = f32[4096,512]{1,0:T(8,128)} fusion(f32[64,512]{1,0:T(8,128)S(1)} %multiply_add_fusion.1, s32[4096]{0:T(1024)S(1)} %fusion.166), kind=kCustom, calls=%fused_computation.clone | custom fusion | bytes 16793600 | tf_op jit(solution)/shard_map/jit(_take)/gather | solution.py:97
  300.2 6.3 %fusion.64 = bf16[256,512]{1,0:T(8,128)(2,1)} fusion(f32[4096,512]{1,0:T(8,128)} %gather_fusion, f32[4096]{0:T(1024)S(1)} %copy-done.10, f32[4096]{0:T(1024)S(1)} %copy-done.11, pred[4096]{0:T(1024)(128)(4,1)S(1)} %get-tuple-element.42, s32[4096]{0:T(1024)S(1)} %copy-done.3), kind=kOutput, calls=%fused_computation.77 | convolution fusion | flops 1083310080 | bytes 8704000 | tf_op jit(solution)/shard_map/dot_general | solution.py:89
  306.6 77.5 %all-reduce.3.cloned.1.call-done = (bf16[256,512]{1,0:T(8,128)(2,1)}, bf16[256,512]{1,0:T(8,128)(2,1)}, bf16[256,512]{1,0:T(8,128)(2,1)}, bf16[256,512]{1,0:T(8,128)(2,1)}) async-done(((bf16[256,512]{1,0:T(8,128)(2,1)}, bf16[256,512]{1,0:T(8,128)(2,1)}, bf16[256,512]{1,0:T(8,128)(2,1)}, bf16[256,512]{1,0:T(8,128)(2,1)}), (bf16[256,512]{1,0:T(8,128)(2,1)}, bf16[256,512]{1,0:T(8,128)(2,1)}, ...) | async-done | bytes 1048592 | tf_op jit(solution)/shard_map/psum | solution.py:90
  384.0 2.5 fusion.38
  387.5 6.0 %constant_dynamic-update-slice_fusion.7 = (bf16[512,512]{1,0:T(8,128)(2,1)}, bf16[64,512]{1,0:T(8,128)(2,1)S(1)}, f32[64,512]{1,0:T(8,128)S(1)}) fusion(f32[4096,512]{1,0:T(8,128)S(1)} %fusion.38, f32[4096,512]{1,0:T(8,128)S(1)} %copy-done.1, f32[4096]{0:T(1024)S(1)} %copy-done.10, f32[4096]{0:T(1024)S(1)} %copy-done.11, ...), kind=kOutput, calls=%fused_computation.196 | convolution fusion | flops 1623523328 | bytes 17092608 | tf_op jit(solution)/shard_map/dot_general | solution.py:106
  397.8 4.0 all-to-all-start
  401.9 4.6 fusion.36
  406.5 9.5 %all-to-all-done = bf16[8,64,512]{2,1,0:T(8,128)(2,1)S(1)} async-done(((bf16[8,64,512]{2,1,0:T(8,128)(2,1)}), bf16[8,64,512]{2,1,0:T(8,128)(2,1)S(1)}, u32[]{:S(2)}, u32[]{:S(2)}) %all-to-all-start) | async-done | bytes 524320 | tf_op jit(solution)/shard_map/all_to_all | solution.py:16
  416.3 9.8 %constant_dynamic-update-slice_fusion.15 = (bf16[512,512]{1,0:T(8,128)(2,1)}, bf16[64,512]{1,0:T(8,128)(2,1)S(1)}, f32[64,512]{1,0:T(8,128)S(1)}) fusion(f32[4096,512]{1,0:T(8,128)} %fusion.36, f32[4096,512]{1,0:T(8,128)} %gather_fusion.1, f32[4096]{0:T(1024)S(1)} %copy-done.10, f32[4096]{0:T(1024)S(1)} %copy-done.11, ...), kind=kOutput, calls=%fused_computation.204 | convolution fusion | flops 1623851008 | bytes 17486848 | tf_op jit(solution)/shard_map/dot_general | solution.py:106
  430.5 3.6 all-to-all-start.1
  434.2 4.6 fusion.34
  438.8 9.7 %all-to-all-done.1 = bf16[8,64,512]{2,1,0:T(8,128)(2,1)S(1)} async-done(((bf16[8,64,512]{2,1,0:T(8,128)(2,1)}), bf16[8,64,512]{2,1,0:T(8,128)(2,1)S(1)}, u32[]{:S(2)}, u32[]{:S(2)}) %all-to-all-start.1) | async-done | bytes 524320 | tf_op jit(solution)/shard_map/all_to_all | solution.py:16
  448.9 9.8 %constant_dynamic-update-slice_fusion.23 = (bf16[512,512]{1,0:T(8,128)(2,1)}, bf16[64,512]{1,0:T(8,128)(2,1)S(1)}, f32[64,512]{1,0:T(8,128)S(1)}) fusion(f32[4096,512]{1,0:T(8,128)} %fusion.34, f32[4096,512]{1,0:T(8,128)} %gather_fusion.2, f32[4096]{0:T(1024)S(1)} %copy-done.10, f32[4096]{0:T(1024)S(1)} %copy-done.11, ...), kind=kOutput, calls=%fused_computation.212 | convolution fusion | flops 1623851008 | bytes 17486848 | tf_op jit(solution)/shard_map/dot_general | solution.py:106
  463.1 3.6 all-to-all-start.2
  466.8 4.6 fusion.32
  471.4 10.0 %all-to-all-done.2 = bf16[8,64,512]{2,1,0:T(8,128)(2,1)S(1)} async-done(((bf16[8,64,512]{2,1,0:T(8,128)(2,1)}), bf16[8,64,512]{2,1,0:T(8,128)(2,1)S(1)}, u32[]{:S(2)}, u32[]{:S(2)}) %all-to-all-start.2) | async-done | bytes 524320 | tf_op jit(solution)/shard_map/all_to_all | solution.py:16
  481.8 9.2 %constant_dynamic-update-slice_fusion.31 = (bf16[512,512]{1,0:T(8,128)(2,1)S(1)}, bf16[64,512]{1,0:T(8,128)(2,1)S(1)}, f32[64,512]{1,0:T(8,128)S(1)}) fusion(f32[4096,512]{1,0:T(8,128)} %fusion.32, f32[4096,512]{1,0:T(8,128)} %gather_fusion.3, f32[4096]{0:T(1024)S(1)} %copy-done.10, f32[4096]{0:T(1024)S(1)} %copy-done.11, ...), kind=kOutput, calls=%fused_computation.220 | convolution fusion | flops 1623851008 | bytes 17486848 | tf_op jit(solution)/shard_map/dot_general | solution.py:106
  491.2 18.1 %all_to_all.48 = bf16[8,64,512]{2,1,0:T(8,128)(2,1)S(1)} all-to-all(bf16[8,64,512]{2,1,0:T(8,128)(2,1)S(1)} %bitcast.97), channel_id=1, replica_groups=mesh['paths'=4,'factors'=8] {'factors'}, dimensions={0} | all-to-all | bytes 1048576 | tf_op jit(solution)/shard_map/all_to_all | solution.py:16
  509.3 1.6 fusion.100
  511.1 38.7 %psum.39 = f32[3,64]{1,0:T(4,128)S(1)} all-reduce(f32[3,64]{1,0:T(4,128)S(1)} %fusion.161), channel_id=1, replica_groups=mesh['paths'=4,'factors'=8] {'paths','factors'}, use_global_device_ids=true, to_apply=%region_20.22 | all-reduce | flops 192 | bytes 1536 | tf_op jit(solution)/shard_map/psum | solution.py:160
  (87 shorter events, 31.6 us)
Async XLA Ops:
  7.2 2.8 copy-start
  7.2 142.6 %copy-start.2 = (f32[4,64,512]{2,1,0:T(8,128)S(1)}, f32[4,64,512]{2,1,0:T(8,128)}, u32[]{:S(2)}) copy-start(f32[4,64,512]{2,1,0:T(8,128)} %param.16) | copy-start | bytes 1572868
  7.2 145.2 %copy-start.8 = (s32[4096]{0:T(1024)S(1)}, s32[4096]{0:T(1024)}, u32[]{:S(2)}) copy-start(s32[4096]{0:T(1024)} %param.26) | copy-start | bytes 49156
  7.2 73.6 %reduce-scatter.13.cloned.1.call-start = ((), (), s32[]{:S(2)}) async-start(), calls=%async_computation.8 | async-start | bytes 1179648 | tf_op jit(solution)/shard_map/reduce_scatter | solution.py:78
  13.5 135.4 %reduce-scatter.15.cloned.1.call-start = ((), (), s32[]{:S(2)}) async-start(), calls=%async_computation.9 | async-start | bytes 1179648 | tf_op jit(solution)/shard_map/reduce_scatter | solution.py:78
  85.2 130.4 %reduce-scatter.17.cloned.1.call-start = ((), (), s32[]{:S(2)}) async-start(), calls=%async_computation.10 | async-start | bytes 1179648 | tf_op jit(solution)/shard_map/reduce_scatter | solution.py:78
  152.4 130.0 %reduce-scatter.19.cloned.1.call-start = ((), (), s32[]{:S(2)}) async-start(), calls=%async_computation.11 | async-start | bytes 1179648 | tf_op jit(solution)/shard_map/reduce_scatter | solution.py:78
  152.5 67.0 %copy-start.3 = (s32[4096]{0:T(1024)S(1)}, s32[4096]{0:T(1024)}, u32[]{:S(2)}) copy-start(s32[4096]{0:T(1024)} %param.25) | copy-start | bytes 49156
  152.5 67.0 %copy-start.10 = (f32[4096]{0:T(1024)S(1)}, f32[4096]{0:T(1024)}, u32[]{:S(2)}) copy-start(f32[4096]{0:T(1024)} %param.24) | copy-start | bytes 49156
  152.5 67.0 %copy-start.11 = (f32[4096]{0:T(1024)S(1)}, f32[4096]{0:T(1024)}, u32[]{:S(2)}) copy-start(f32[4096]{0:T(1024)} %param.23) | copy-start | bytes 49156
  219.2 164.8 %all-reduce.3.cloned.1.call-start = ((), (), s32[]{:S(2)}) async-start(), calls=%async_computation.12 | async-start | bytes 2097152 | tf_op jit(solution)/shard_map/psum | solution.py:90
  300.2 6.4 %copy-start.9 = (f32[256]{0:T(256)S(1)}, f32[256]{0:T(256)}, u32[]{:S(2)}) copy-start(f32[256]{0:T(256)} %param.27) | copy-start | bytes 3076
  384.0 3.5 copy-start.1
  387.5 14.4 %copy-start.7 = (bf16[256,512]{1,0:T(8,128)(2,1)S(1)}, bf16[256,512]{1,0:T(8,128)(2,1)}, u32[]{:S(2)}) copy-start(bf16[256,512]{1,0:T(8,128)(2,1)} %get-tuple-element.30) | copy-start | bytes 786436
  397.8 18.1 %all-to-all-start = ((bf16[8,64,512]{2,1,0:T(8,128)(2,1)}), bf16[8,64,512]{2,1,0:T(8,128)(2,1)S(1)}, u32[]{:S(2)}, u32[]{:S(2)}) async-start(bf16[8,64,512]{2,1,0:T(8,128)(2,1)} %bitcast.14), calls=%async_computation | async-start | bytes 1048576 | tf_op jit(solution)/shard_map/all_to_all | solution.py:16
  416.3 17.8 %copy-start.6 = (bf16[256,512]{1,0:T(8,128)(2,1)S(1)}, bf16[256,512]{1,0:T(8,128)(2,1)}, u32[]{:S(2)}) copy-start(bf16[256,512]{1,0:T(8,128)(2,1)} %get-tuple-element.29) | copy-start | bytes 786436
  430.5 18.0 %all-to-all-start.1 = ((bf16[8,64,512]{2,1,0:T(8,128)(2,1)}), bf16[8,64,512]{2,1,0:T(8,128)(2,1)S(1)}, u32[]{:S(2)}, u32[]{:S(2)}) async-start(bf16[8,64,512]{2,1,0:T(8,128)(2,1)} %bitcast.17), calls=%async_computation.1 | async-start | bytes 1048576 | tf_op jit(solution)/shard_map/all_to_all | solution.py:16
  448.9 17.9 %copy-start.5 = (bf16[256,512]{1,0:T(8,128)(2,1)S(1)}, bf16[256,512]{1,0:T(8,128)(2,1)}, u32[]{:S(2)}) copy-start(bf16[256,512]{1,0:T(8,128)(2,1)} %get-tuple-element.28) | copy-start | bytes 786436
  463.1 18.3 %all-to-all-start.2 = ((bf16[8,64,512]{2,1,0:T(8,128)(2,1)}), bf16[8,64,512]{2,1,0:T(8,128)(2,1)S(1)}, u32[]{:S(2)}, u32[]{:S(2)}) async-start(bf16[8,64,512]{2,1,0:T(8,128)(2,1)} %bitcast.20), calls=%async_computation.2 | async-start | bytes 1048576 | tf_op jit(solution)/shard_map/all_to_all | solution.py:16
  481.8 27.5 %copy-start.4 = (f32[64,512]{1,0:T(8,128)S(1)}, f32[64,512]{1,0:T(8,128)}, u32[]{:S(2)}) copy-start(f32[64,512]{1,0:T(8,128)} %param.15) | copy-start | bytes 393220
  481.8 29.1 %copy-start.12 = (s32[64]{0:T(128)S(1)}, s32[64]{0:T(128)}, u32[]{:S(2)}) copy-start(s32[64]{0:T(128)} %param.22) | copy-start | bytes 772
Sparse Core Ops, SparseCore 0:
  13.6 67.1 reduce-scatter.12
  85.3 63.4 reduce-scatter.14
  152.5 63.1 reduce-scatter.16
  219.3 63.0 reduce-scatter.18
  306.7 77.3 all-reduce.2
